TPU v7x, 32 devices: a whole 2x2x4 slice. The times are simulated.
32 devices in a mesh: sec: 2 (over core), grp: 4 (over y, x), dev: 4 (over z).
Axes of the slice: x: 2, y: 2, z: 4, core: 2. Of those that a mesh axis runs over, the one named last changes fastest.
Arguments:
- current: float32 [32, 196608], P(None, ('sec', 'grp', 'dev')), may hold values from -6 to 6
- prior: float32 [8, 32, 196608], P(None, None, ('sec', 'grp', 'dev')), as said below
- block_values: float32 [1024, 6, 9216], P(('grp', 'dev')), may hold values from -0.25 to 0.25
- block_cols: int32 [1024, 6], P(('grp', 'dev')), may hold values from 0 to 63
- face_match: int32 [16, 4, 1536], P(('grp', 'dev')), may hold values from 0 to 1535, each once within a row
- face_weight: float32 [16, 4, 1536], P(('grp', 'dev')), may hold values from -3 to 3
- fluid_diag: float32 [98304], P(('grp', 'dev')), may hold values from 2 to 4
- wet_source: int32 [49152], P(('grp', 'dev')), may hold values from 0 to 6143
- wet_dest: int32 [49152, 1], P(('grp', 'dev')), may hold values from 0 to 15; in each aligned block of 3072 rows (0 to 3071, 3072 to 6143, ...) at most 392 rows name the same one
- wet_target: int32 [49152], P(('grp', 'dev')), may hold values from 0 to 6143
- wet_weight: float32 [49152], P(('grp', 'dev')), may hold values from -5 to 5
Outputs:
- next_block: float32 [32, 196608], P(None, ('sec', 'grp', 'dev'))
- coeffs: float32 [8, 32, 32], replicated
- rfac: float32 [32, 32], replicated
Inputs may be any that keep to these rules, and one draw needn't show every extreme that they name: `block_cols`: block columns index blocks within the same subdomain. `face_match`: each subdomain's matching of one round is a permutation of its face. `prior`: each earlier block's columns have about unit length. `wet_dest`: among one structure subdomain's couplings, at most 392 name the same fluid subdomain, and some subdomain has exactly 392 for one.
All inputs are finite; a program needn't handle non-finite values.
Results may differ from a plain program's by a relative error of at most 0.00008.
Values sent between devices are 32-bit elements; how exact they have to be, the bound alone decides.
A program may use at most 128 MiB of HBM per device.

v0:
```python
import jax
import jax.numpy as jnp
from jax import lax
from jax.sharding import PartitionSpec as P

BS = 96
NB = 6
ROUNDS = 4


def swapped(block, axis, bit):
    count = lax.axis_size(axis)
    route = []
    for low in range(count):
        high = low | 1 << bit
        if high != low and high < count:
            route += [(low, high), (high, low)]
    return lax.ppermute(block, axis, route)


def with_halo(x, sides, width):
    for axis, dim in sides:
        count, length = (lax.axis_size(axis), x.shape[dim])
        up = [(i, (i + 1) % count) for i in range(count - 1)]
        down = [(j, i) for i, j in up]
        last = lax.slice_in_dim(x, length - width, length, axis=dim)
        initial = lax.slice_in_dim(x, 0, width, axis=dim)
        before = lax.ppermute(last, axis, up)
        after = lax.ppermute(initial, axis, down)
        x = jnp.concatenate([before, x, after], axis=dim)
    return x


def shards(
    current,
    prior,
    block_values,
    block_cols,
    face_match,
    face_weight,
    fluid_diag,
    wet_source,
    wet_dest,
    wet_target,
    wet_weight,
):
    highest = lax.Precision.HIGHEST
    width = current.shape[0]
    local_rows = current.shape[1]
    face_rows = face_match.shape[2]
    row_blocks = block_cols.shape[0]
    wet_slots = wet_source.shape[0]
    subdomains = lax.axis_size("grp") * lax.axis_size("dev")
    total_rows = local_rows * lax.axis_size("sec") * subdomains
    capacity = 2 * wet_slots // subdomains + 8
    is_shell = lax.axis_index("sec") == 0
    senders = jnp.where(is_shell, 1.0, 0.0).astype(jnp.float32)
    partner_faces = []
    for sweep in range(ROUNDS):
        face_now = current[:, sweep * face_rows : (sweep + 1) * face_rows]
        if sweep < 2:
            partner_faces.append(swapped(face_now, "dev", sweep))
        else:
            partner_faces.append(swapped(face_now, "grp", sweep - 2))
    padded = with_halo(current, ((("grp", "dev"), 1),), 1)
    destination = wet_dest[:, 0]
    onehot = (destination[:, None] == jnp.arange(subdomains, dtype=jnp.int32)[None, :]).astype(
        jnp.int32
    )
    ranks = jnp.cumsum(onehot, axis=0) - 1
    slot = jnp.sum(ranks * onehot, axis=1)
    moved = (wet_weight * senders)[None, :] * current[:, wet_source]
    target_float = wet_target.astype(jnp.float32) * senders
    buffer = jnp.zeros((2 * subdomains, width, capacity), jnp.float32)
    buffer = buffer.at[destination + subdomains, :, slot].set(moved.T)
    row_buffer = jnp.zeros((2 * subdomains, capacity), jnp.float32)
    row_buffer = row_buffer.at[destination + subdomains, slot].set(target_float)
    got_values, got_rows = (
        lax.all_to_all(buffer, ("sec", "grp", "dev"), split_axis=0, concat_axis=0, tiled=True),
        lax.all_to_all(row_buffer, ("sec", "grp", "dev"), split_axis=0, concat_axis=0, tiled=True),
    )
    incoming = jnp.moveaxis(got_values, 1, 0).reshape(width, -1)
    incoming_rows = got_rows.reshape(-1).astype(jnp.int32)

    def shell_apply(vector):
        picked = vector.reshape(width, row_blocks, BS)[:, block_cols, :]
        matrices = block_values.reshape(row_blocks, NB, BS, BS)
        result = jnp.einsum("kibc,ibrc->kir", picked, matrices, precision=highest).reshape(
            width, local_rows
        )
        for sweep in range(ROUNDS):
            matched = partner_faces[sweep][:, face_match[0, sweep]]
            result = result.at[:, sweep * face_rows : (sweep + 1) * face_rows].add(
                face_weight[0, sweep][None, :] * matched
            )
        return result

    def fluid_apply(vector):
        before = padded[:, :-2]
        after = padded[:, 2:]
        result = fluid_diag[None, :] * vector - before - after
        return result.at[:, incoming_rows].add(incoming)

    image = lax.cond(is_shell, shell_apply, fluid_apply, current)
    h_first = lax.psum(
        jnp.einsum("jkr,lr->jkl", prior, image, precision=highest), ("sec", "grp", "dev")
    )
    w_one = image - jnp.einsum("jkl,jkr->lr", h_first, prior, precision=highest)
    h_second = lax.psum(
        jnp.einsum("jkr,lr->jkl", prior, w_one, precision=highest), ("sec", "grp", "dev")
    )
    w_two = w_one - jnp.einsum("jkl,jkr->lr", h_second, prior, precision=highest)
    gram = lax.psum(jnp.dot(w_two, w_two.T, precision=highest), ("sec", "grp", "dev")) / total_rows
    coeffs = h_first + h_second
    factor = jnp.linalg.cholesky(gram)
    next_block = lax.linalg.triangular_solve(factor, w_two, left_side=True, lower=True)
    return (next_block, coeffs, factor.T)


def solution(mesh):
    placed = (
        P(None, ("sec", "grp", "dev")),
        P(None, None, ("sec", "grp", "dev")),
        P(("grp", "dev"), None, None),
        P(("grp", "dev"), None),
        P(("grp", "dev"), None, None),
        P(("grp", "dev"), None, None),
        P(("grp", "dev")),
        P(("grp", "dev")),
        P(("grp", "dev"), None),
        P(("grp", "dev")),
        P(("grp", "dev")),
    )
    return jax.shard_map(
        shards,
        mesh=mesh,
        in_specs=placed,
        out_specs=(P(None, ("sec", "grp", "dev")), P(), P()),
        check_vma=False,
    )
```

profile of v0, /device:TPU:0, one launch (start us, length us, event | category | flops | bytes accessed | tf_op | source)
XLA Modules:
  0.0 426.9 jit_solution(6008046726579395630)
XLA Ops:
  1.4 4.6 %reduce-window.6 = s32[16,24,128]{2,1,0:T(8,128)S(1)} reduce-window(s32[16,24,128]{2,1,0:T(8,128)S(1)} %fusion.27, s32[]{:T(128)} %constant.179.clone.1), window={size=1x1x128 pad=0_0x0_0x127_0}, to_apply=%region_0.1 | reduce-window | flops 6242304 | bytes 393220 | tf_op jit(solution)/shard_map/reduce-window
  6.7 0.8 fusion.26
  8.2 0.8 and_reduce_fusion
  10.5 11.8 %scatter_custom_fusion.1 = f32[12544]{0:T(1024)S(1)} fusion(s32[3072]{0:T(1024)S(1)} %broadcast_select_fusion, f32[3072]{0:T(1024)S(1)} %get-tuple-element.233, f32[]{:T(128)} %constant.180.clone.1), kind=kCustom, calls=%fused_computation.71 | custom fusion | bytes 50180
  22.3 0.8 all_to_all.9
  23.1 7.3 %all-to-all-start = ((f32[32,1,392]{2,1,0:T(1,128)}), f32[32,1,392]{2,1,0:T(1,128)S(1)}, u32[]{:S(2)}, u32[]{:S(2)}) async-start(f32[32,1,392]{2,1,0:T(1,128)} %all_to_all.9), calls=%async_computation | async-start | bytes 131072 | tf_op jit(solution)/shard_map/all_to_all | solution.py:80
  31.2 2.0 copy.123
  33.1 20.8 %scatter_custom_fusion.2 = f32[12544,32]{1,0:T(8,128)} fusion(s32[3072]{0:T(1024)S(1)} %broadcast_select_fusion, f32[]{:T(128)} %constant.180.clone.1, f32[3072]{0:T(1024)S(1)} %get-tuple-element.234, f32[32,6144]{0,1:T(8,128)S(1)} %copy.123, s32[3072]{0:T(1024)S(1)} %fusion.34), kind=kCustom, calls=%fused_computation.50 | custom fusion | flops 98304 | bytes 4775940
  53.9 6.0 %copy.125 = f32[32,32,392]{2,1,0:T(8,128)} copy(f32[32,32,392]{1,2,0:T(8,128)} %bitcast.92) | data formatting | bytes 3211264 | tf_op jit(solution)/shard_map/scatter | solution.py:75
  60.0 5.8 %all-to-all-start.1 = ((f32[32,32,392]{2,1,0:T(8,128)}), f32[32,32,392]{2,1,0:T(8,128)S(1)}, u32[]{:S(2)}, u32[]{:S(2)}) async-start(f32[32,32,392]{2,1,0:T(8,128)} %copy.125), calls=%async_computation.1 | async-start | bytes 4194304 | tf_op jit(solution)/shard_map/all_to_all | solution.py:79
  65.9 0.8 fusion.36
  66.7 1.8 collective-permute-start.2
  68.4 2.4 collective-permute-start.3
  70.8 1.5 collective-permute-start.4
  72.3 1.5 collective-permute-start.5
  73.9 2.4 collective-permute-start
  76.3 33.0 %collective-permute-done = f32[32,1]{1,0:T(8,128)S(1)} collective-permute-done((f32[32,1]{1,0:T(8,128)S(1)}, f32[32,1]{1,0:T(8,128)S(1)}, u32[]{:S(2)}, u32[]{:S(2)}) %collective-permute-start) | collective-permute-done | bytes 160 | tf_op jit(solution)/shard_map/ppermute | solution.py:28
  109.3 1.3 collective-permute-start.1
  110.6 15.2 %collective-permute-done.1 = f32[32,1]{1,0:T(8,128)S(1)} collective-permute-done((f32[32,1]{1,0:T(8,128)S(1)}, f32[32,1]{1,0:T(8,128)S(1)}, u32[]{:S(2)}, u32[]{:S(2)}) %collective-permute-start.1) | collective-permute-done | bytes 160 | tf_op jit(solution)/shard_map/ppermute | solution.py:29
  125.8 1.2 concatenate.15
  127.1 81.7 %conditional.1 = (f32[32,6144]{0,1:T(8,128)}) conditional(s32[]{:T(128)} %convert_element_type.23, (f32[6144]{0:T(1024)S(1)}, f32[32,6144]{1,0:T(8,128)S(1)}, f32[32,6146]{1,0:T(8,128)}, f32[32,1,392]{2,1,0:T(1,128)S(1)}, f32[32,32,392]{2,0,1:T(8,128)S(1)}) %tuple.73, (f32[32,6144]{1,0:T(8,128)S(1)}, s32[64,6]{0,1:T(8,128)S(1)}, ...), branch_computations={%region_5.7_spmd, %region_7.11_spmd} | conditional | flops 1359523968 | bytes 72574472 | solution.py:104
  135.6 3.8 gather_fusion
  139.4 17.6 %reshape.288 = f32[64,6,96,96]{3,2,0,1:T(8,128)} reshape(f32[64,6,9216]{2,0,1:T(8,128)} %get-tuple-element.106) | data formatting | bytes 28311552 | tf_op jit(solution)/shard_map/cond/branch_1_fun/reshape | solution.py:87
  157.0 20.7 %fusion.2 = f32[32,64,96]{2,0,1:T(8,128)S(1)} fusion(f32[32,64,6,96]{3,0,2,1:T(8,128)} %bitcast.91, f32[64,6,96,96]{3,2,0,1:T(8,128)} %reshape.288), kind=kOutput, calls=%fused_computation.11 | convolution fusion | flops 1358954496 | bytes 19660800 | tf_op jit(solution)/shard_map/cond/branch_1_fun/kibc,ibrc->kir/dot_general | solution.py:88
  177.7 2.3 copy.146
  180.0 1.2 copy.130
  181.3 2.6 gather_fusion.1
  184.6 2.9 fusion.5
  187.6 1.2 copy.131
  188.8 2.6 gather_fusion.2
  192.0 2.9 fusion.6
  194.9 1.2 copy.132
  196.1 2.6 gather_fusion.3
  199.4 3.0 fusion.7
  202.4 1.2 copy.133
  203.6 2.6 gather_fusion.4
  206.2 2.4 fusion.8
  208.7 2.3 copy.135
  211.1 22.2 %fusion.20 = f32[8,32,32]{1,2,0:T(8,128)S(1)} fusion(f32[8,32,6144]{2,1,0:T(8,128)} %param.22, f32[32,6144]{0,1:T(8,128)} %get-tuple-element.235), kind=kOutput, calls=%fused_computation.56 | convolution fusion | flops 603979776 | bytes 7110656 | tf_op jit(solution)/shard_map/jkr,lr->jkl/dot_general | solution.py:106
  233.2 70.2 %psum.21 = f32[8,32,32]{1,2,0:T(8,128)S(1)} all-reduce(f32[8,32,32]{1,2,0:T(8,128)S(1)} %fusion.20), channel_id=1, replica_groups=mesh['sec'=2,'grp'=4,'dev'=4] {'sec','grp','dev'}, use_global_device_ids=true, to_apply=%region_11.12 | all-reduce | flops 8192 | bytes 65536 | tf_op jit(solution)/shard_map/psum | solution.py:105
  303.4 7.5 %convolution_bitcast_fusion.1 = f32[32,6144]{1,0:T(8,128)S(1)} fusion(f32[8,32,32]{1,2,0:T(8,128)S(1)} %psum.21, f32[8,32,6144]{2,1,0:T(8,128)} %param.22), kind=kOutput, calls=%fused_computation.48 | convolution fusion | flops 603979776 | bytes 7110656 | tf_op jit(solution)/shard_map/jkl,jkr->lr/dot_general | solution.py:108
  311.1 16.3 %convolution_bitcast_fusion.2 = f32[8,32,32]{1,2,0:T(8,128)S(1)} fusion(f32[8,32,6144]{2,1,0:T(8,128)} %param.22, f32[32,6144]{1,0:T(8,128)S(1)} %sub.23), kind=kOutput, calls=%fused_computation.55 | convolution fusion | flops 603979776 | bytes 7110656 | tf_op jit(solution)/shard_map/jkr,lr->jkl/dot_general | solution.py:110
  327.4 41.1 %psum.22 = f32[8,32,32]{1,2,0:T(8,128)S(1)} all-reduce(f32[8,32,32]{1,2,0:T(8,128)S(1)} %convolution_bitcast_fusion.2), channel_id=1, replica_groups=mesh['sec'=2,'grp'=4,'dev'=4] {'sec','grp','dev'}, use_global_device_ids=true, to_apply=%region_12.13 | all-reduce | flops 8192 | bytes 65536 | tf_op jit(solution)/shard_map/psum | solution.py:109
  368.5 7.6 %fusion.14 = f32[32,6144]{1,0:T(8,128)S(1)} fusion(f32[32,6144]{1,0:T(8,128)S(1)} %sub.23, f32[8,32,32]{1,2,0:T(8,128)S(1)} %psum.22, f32[8,32,6144]{2,1,0:T(8,128)} %param.22), kind=kOutput, calls=%fused_computation.49 | convolution fusion | flops 604176384 | bytes 7897088 | tf_op jit(solution)/shard_map/jkl,jkr->lr/dot_general | solution.py:112
  376.8 39.9 %psum.23 = f32[32,32]{0,1:T(8,128)S(1)} all-reduce(f32[32,32]{0,1:T(8,128)S(1)} %fusion.38), channel_id=1, replica_groups=mesh['sec'=2,'grp'=4,'dev'=4] {'sec','grp','dev'}, use_global_device_ids=true, to_apply=%region_13.14 | all-reduce | flops 1024 | bytes 8192 | tf_op jit(solution)/shard_map/psum | solution.py:113
  416.8 2.9 cholesky.16
  421.1 2.4 custom-call.6
  423.5 1.7 fusion.30
  (50 shorter events, 11.6 us)
Async XLA Ops:
  23.1 36.9 %all-to-all-start = ((f32[32,1,392]{2,1,0:T(1,128)}), f32[32,1,392]{2,1,0:T(1,128)S(1)}, u32[]{:S(2)}, u32[]{:S(2)}) async-start(f32[32,1,392]{2,1,0:T(1,128)} %all_to_all.9), calls=%async_computation | async-start | bytes 131072 | tf_op jit(solution)/shard_map/all_to_all | solution.py:80
  60.0 5.9 %copy-start = (f32[32,6144]{1,0:T(8,128)S(1)}, f32[32,6144]{1,0:T(8,128)}, u32[]{:S(2)}) copy-start(f32[32,6144]{1,0:T(8,128)} %param.21) | copy-start | bytes 2359300
  60.0 67.0 %copy-start.3 = (f32[1,4,1536]{2,1,0:T(4,128)S(1)}, f32[1,4,1536]{2,1,0:T(4,128)}, u32[]{:S(2)}) copy-start(f32[1,4,1536]{2,1,0:T(4,128)} %param.26) | copy-start | bytes 73732
  60.0 67.0 %copy-start.4 = (s32[1,4,1536]{2,1,0:T(4,128)S(1)}, s32[1,4,1536]{2,1,0:T(4,128)}, u32[]{:S(2)}) copy-start(s32[1,4,1536]{2,1,0:T(4,128)} %param.25) | copy-start | bytes 73732
  60.0 67.1 %copy-start.5 = (f32[6144]{0:T(1024)S(1)}, f32[6144]{0:T(1024)}, u32[]{:S(2)}) copy-start(f32[6144]{0:T(1024)} %param.27) | copy-start | bytes 73732
  60.0 67.1 %copy-start.6 = (s32[64,6]{0,1:T(8,128)S(1)}, s32[64,6]{0,1:T(8,128)}, u32[]{:S(2)}) copy-start(s32[64,6]{0,1:T(8,128)} %param.24) | copy-start | bytes 4612
  60.0 67.0 %all-to-all-start.1 = ((f32[32,32,392]{2,1,0:T(8,128)}), f32[32,32,392]{2,1,0:T(8,128)S(1)}, u32[]{:S(2)}, u32[]{:S(2)}) async-start(f32[32,32,392]{2,1,0:T(8,128)} %copy.125), calls=%async_computation.1 | async-start | bytes 4194304 | tf_op jit(solution)/shard_map/all_to_all | solution.py:79
  66.7 60.3 %collective-permute-start.2 = (f32[32,1536]{1,0:T(8,128)}, f32[32,1536]{1,0:T(8,128)}, u32[]{:S(2)}, u32[]{:S(2)}) collective-permute-start(f32[32,1536]{1,0:T(8,128)} %get-tuple-element.226), channel_id=1, source_target_pairs={{0,1},{1,0},{2,3},{3,2},{4,5},{5,4},{6,7},{7,6},{8,9},{9,8},{10,11... | collective-permute-start | bytes 589832 | tf_op jit(solution)/shard_map/ppermute | solution.py:18
  68.4 58.6 %collective-permute-start.3 = (f32[32,1536]{1,0:T(8,128)}, f32[32,1536]{1,0:T(8,128)}, u32[]{:S(2)}, u32[]{:S(2)}) collective-permute-start(f32[32,1536]{1,0:T(8,128)} %get-tuple-element.225), channel_id=1, source_target_pairs={{0,2},{2,0},{1,3},{3,1},{4,6},{6,4},{5,7},{7,5},{8,10},{10,8},{9,1... | collective-permute-start | bytes 589832 | tf_op jit(solution)/shard_map/ppermute | solution.py:18
  70.8 56.1 %collective-permute-start.4 = (f32[32,1536]{1,0:T(8,128)S(1)}, f32[32,1536]{1,0:T(8,128)}, u32[]{:S(2)}, u32[]{:S(2)}) collective-permute-start(f32[32,1536]{1,0:T(8,128)S(1)} %get-tuple-element.224), channel_id=1, source_target_pairs={{0,4},{4,0},{8,12},{12,8},{1,5},{5,1},{9,13},{13,9},{2,6},{6,2},{1... | collective-permute-start | bytes 589832 | tf_op jit(solution)/shard_map/ppermute | solution.py:18
  72.3 54.7 %collective-permute-start.5 = (f32[32,1536]{1,0:T(8,128)S(1)}, f32[32,1536]{1,0:T(8,128)}, u32[]{:S(2)}, u32[]{:S(2)}) collective-permute-start(f32[32,1536]{1,0:T(8,128)S(1)} %get-tuple-element.223), channel_id=1, source_target_pairs={{0,8},{8,0},{4,12},{12,4},{1,9},{9,1},{5,13},{13,5},{2,10},{10,2},... | collective-permute-start | bytes 589832 | tf_op jit(solution)/shard_map/ppermute | solution.py:18
  73.9 35.4 %collective-permute-start = (f32[32,1]{1,0:T(8,128)S(1)}, f32[32,1]{1,0:T(8,128)S(1)}, u32[]{:S(2)}, u32[]{:S(2)}) collective-permute-start(f32[32,1]{1,0:T(8,128)S(1)} %get-tuple-element.228), channel_id=1, source_target_pairs={{0,1},{1,2},{2,3},{3,4},{4,5},{5,6},{6,7},{7,8},{8,9},{9,10},{10,1... | collective-permute-start | bytes 392 | tf_op jit(solution)/shard_map/ppermute | solution.py:28
  109.3 16.5 %collective-permute-start.1 = (f32[32,1]{1,0:T(8,128)S(1)}, f32[32,1]{1,0:T(8,128)S(1)}, u32[]{:S(2)}, u32[]{:S(2)}) collective-permute-start(f32[32,1]{1,0:T(8,128)S(1)} %get-tuple-element.227), channel_id=1, source_target_pairs={{1,0},{2,1},{3,2},{4,3},{5,4},{6,5},{7,6},{8,7},{9,8},{10,9},{11,1... | collective-permute-start | bytes 392 | tf_op jit(solution)/shard_map/ppermute | solution.py:29
where the time goes:
time: 434 us; the launch traced here: 427 us
  blocking collectives  151 us (35%)
  matrix products  76.7 us (18%)
  local copies, waits for them, and re-layouts  67.1 us (15%)
  other arithmetic  51 us (12%)
  waiting for transfers between devices  48.2 us (11%)
  starting transfers between devices  24 us (6%)
  loops' own time  7.54 us (2%)
    psum x1, blocking collectives, shards(): lax.psum(jnp.einsum('jkr,lr->jkl', prior, image, precision=highest), ('se...  70.2 us
    psum x1, blocking collectives, shards(): lax.psum(jnp.einsum('jkr,lr->jkl', prior, w_one, precision=highest), ('se...  41.1 us
    psum x1, blocking collectives, shards(): lax.psum(jnp.dot(w_two, w_two.T, precision=highest), ('sec', 'grp', 'dev'))  39.9 us
    ppermute x1, waiting for transfers between devices, with_halo(): before = lax.ppermute(last, axis, up)  33 us
    unnamed x4, other arithmetic  22.4 us
    dot_general x1, matrix products, shards(): jnp.einsum('jkr,lr->jkl', prior, image, precision=highest)  22.2 us
    dot_general x1, matrix products, shell_apply(): jnp.einsum('kibc,ibrc->kir', picked, matrices, precision=highest)  20.7 us
    reshape x1, local copies, waits for them, and re-layouts, shell_apply(): matrices = block_values.reshape(row_blocks, NB, BS, BS)  17.6 us
  transfers between devices with their start and end apart: 8, of which 2 were waited for; matrix products, arithmetic and copies ran while one was open for 7% of the time, Pallas kernels for 0%

commit v1 on v0

--- a/solution.py
+++ b/solution.py
@@ -110,7 +110,13 @@
         jnp.einsum("jkr,lr->jkl", prior, w_one, precision=highest), ("sec", "grp", "dev")
     )
     w_two = w_one - jnp.einsum("jkl,jkr->lr", h_second, prior, precision=highest)
-    gram = lax.psum(jnp.dot(w_two, w_two.T, precision=highest), ("sec", "grp", "dev")) / total_rows
+    gram = (
+        jnp.sum(
+            lax.all_gather(jnp.dot(w_two, w_two.T, precision=highest), ("sec", "grp", "dev")),
+            axis=0,
+        )
+        / total_rows
+    )
     coeffs = h_first + h_second
     factor = jnp.linalg.cholesky(gram)
     next_block = lax.linalg.triangular_solve(factor, w_two, left_side=True, lower=True)

time: 434 us -> 471 us (1.085)
  the two profiles are of different devices: /device:TPU:0 before, /device:TPU:4 now
where the time goes in v1:
time: 471 us; the launch traced here: 464 us
  blocking collectives  190 us (40%)
  matrix products  76.8 us (16%)
  local copies, waits for them, and re-layouts  67.1 us (14%)
  other arithmetic  51.1 us (11%)
  waiting for transfers between devices  48.6 us (10%)
  starting transfers between devices  22.2 us (5%)
  loops' own time  7.54 us (2%)
    all_gather x1, blocking collectives, shards(): lax.all_gather(jnp.dot(w_two, w_two.T, precision=highest), ('sec', 'grp',...  77.8 us
    psum x1, blocking collectives, shards(): lax.psum(jnp.einsum('jkr,lr->jkl', prior, image, precision=highest), ('se...  70.8 us
    psum x1, blocking collectives, shards(): lax.psum(jnp.einsum('jkr,lr->jkl', prior, w_one, precision=highest), ('se...  41.1 us
    ppermute x1, waiting for transfers between devices, with_halo(): before = lax.ppermute(last, axis, up)  38.7 us
    unnamed x4, other arithmetic  22.4 us
    dot_general x1, matrix products, shards(): jnp.einsum('jkr,lr->jkl', prior, image, precision=highest)  22.2 us
    dot_general x1, matrix products, shell_apply(): jnp.einsum('kibc,ibrc->kir', picked, matrices, precision=highest)  20.7 us
    reshape x1, local copies, waits for them, and re-layouts, shell_apply(): matrices = block_values.reshape(row_blocks, NB, BS, BS)  17.6 us
  transfers between devices with their start and end apart: 8, of which 2 were waited for; matrix products, arithmetic and copies ran while one was open for 7% of the time, Pallas kernels for 0%

profile of v1, /device:TPU:4, one launch (start us, length us, event | category | flops | bytes accessed | tf_op | source)
XLA Modules:
  0.0 464.3 jit_solution(9111072276858079551)
XLA Ops:
  1.4 4.6 reduce-window.6
  6.7 0.8 fusion.26
  8.2 0.8 and_reduce_fusion
  9.0 0.8 multiply_reduce_fusion
  10.5 11.8 %scatter_custom_fusion.1 = f32[12544]{0:T(1024)S(1)} fusion(s32[3072]{0:T(1024)S(1)} %broadcast_select_fusion, f32[3072]{0:T(1024)S(1)} %get-tuple-element.233, f32[]{:T(128)} %constant.180.clone.1), kind=kCustom, calls=%fused_computation.71 | custom fusion | bytes 50180
  22.3 0.8 all_to_all.9
  23.1 6.1 %all-to-all-start = ((f32[32,1,392]{2,1,0:T(1,128)}), f32[32,1,392]{2,1,0:T(1,128)S(1)}, u32[]{:S(2)}, u32[]{:S(2)}) async-start(f32[32,1,392]{2,1,0:T(1,128)} %all_to_all.9), calls=%async_computation | async-start | bytes 131072 | tf_op jit(solution)/shard_map/all_to_all | solution.py:80
  29.9 2.0 copy.120
  31.9 20.8 %scatter_custom_fusion.2 = f32[12544,32]{1,0:T(8,128)} fusion(s32[3072]{0:T(1024)S(1)} %broadcast_select_fusion, f32[]{:T(128)} %constant.180.clone.1, f32[3072]{0:T(1024)S(1)} %get-tuple-element.234, f32[32,6144]{0,1:T(8,128)S(1)} %copy.120, s32[3072]{0:T(1024)S(1)} %fusion.34), kind=kCustom, calls=%fused_computation.50 | custom fusion | flops 98304 | bytes 4775940
  52.7 6.0 %copy.122 = f32[32,32,392]{2,1,0:T(8,128)} copy(f32[32,32,392]{1,2,0:T(8,128)} %bitcast.93) | data formatting | bytes 3211264 | tf_op jit(solution)/shard_map/scatter | solution.py:75
  58.8 5.8 %all-to-all-start.1 = ((f32[32,32,392]{2,1,0:T(8,128)}), f32[32,32,392]{2,1,0:T(8,128)S(1)}, u32[]{:S(2)}, u32[]{:S(2)}) async-start(f32[32,32,392]{2,1,0:T(8,128)} %copy.122), calls=%async_computation.1 | async-start | bytes 4194304 | tf_op jit(solution)/shard_map/all_to_all | solution.py:79
  64.6 0.8 fusion.36
  65.4 1.5 collective-permute-start.2
  66.9 2.4 collective-permute-start.3
  69.3 1.5 collective-permute-start.4
  71.4 2.4 collective-permute-start
  73.8 38.7 %collective-permute-done = f32[32,1]{1,0:T(8,128)S(1)} collective-permute-done((f32[32,1]{1,0:T(8,128)S(1)}, f32[32,1]{1,0:T(8,128)S(1)}, u32[]{:S(2)}, u32[]{:S(2)}) %collective-permute-start) | collective-permute-done | bytes 160 | tf_op jit(solution)/shard_map/ppermute | solution.py:28
  112.5 1.9 collective-permute-start.1
  114.4 9.9 %collective-permute-done.1 = f32[32,1]{1,0:T(8,128)S(1)} collective-permute-done((f32[32,1]{1,0:T(8,128)S(1)}, f32[32,1]{1,0:T(8,128)S(1)}, u32[]{:S(2)}, u32[]{:S(2)}) %collective-permute-start.1) | collective-permute-done | bytes 160 | tf_op jit(solution)/shard_map/ppermute | solution.py:29
  124.4 1.2 concatenate.15
  125.7 81.7 %conditional.1 = (f32[32,6144]{0,1:T(8,128)}) conditional(s32[]{:T(128)} %convert_element_type.23, (f32[6144]{0:T(1024)S(1)}, f32[32,6144]{1,0:T(8,128)S(1)}, f32[32,6146]{1,0:T(8,128)}, f32[32,1,392]{2,1,0:T(1,128)S(1)}, f32[32,32,392]{2,0,1:T(8,128)S(1)}) %tuple.73, (f32[32,6144]{1,0:T(8,128)S(1)}, s32[64,6]{0,1:T(8,128)S(1)}, ...), branch_computations={%region_5.7_spmd, %region_7.11_spmd} | conditional | flops 1359523968 | bytes 72574472 | solution.py:104
  134.2 3.8 gather_fusion
  138.0 17.6 %reshape.288 = f32[64,6,96,96]{3,2,0,1:T(8,128)} reshape(f32[64,6,9216]{2,0,1:T(8,128)} %get-tuple-element.106) | data formatting | bytes 28311552 | tf_op jit(solution)/shard_map/cond/branch_1_fun/reshape | solution.py:87
  155.6 20.7 %fusion.2 = f32[32,64,96]{2,0,1:T(8,128)S(1)} fusion(f32[32,64,6,96]{3,0,2,1:T(8,128)} %bitcast.92, f32[64,6,96,96]{3,2,0,1:T(8,128)} %reshape.288), kind=kOutput, calls=%fused_computation.11 | convolution fusion | flops 1358954496 | bytes 19660800 | tf_op jit(solution)/shard_map/cond/branch_1_fun/kibc,ibrc->kir/dot_general | solution.py:88
  176.3 2.3 copy.142
  178.6 1.2 copy.127
  179.9 2.6 gather_fusion.1
  183.3 2.9 fusion.5
  186.2 1.2 copy.128
  187.4 2.6 gather_fusion.2
  190.6 2.9 fusion.6
  193.6 1.2 copy.129
  194.8 2.6 gather_fusion.3
  198.0 3.0 fusion.7
  201.0 1.2 copy.130
  202.2 2.6 gather_fusion.4
  204.8 2.4 fusion.8
  207.3 2.3 copy.132
  209.7 22.2 %fusion.20 = f32[8,32,32]{1,2,0:T(8,128)S(1)} fusion(f32[8,32,6144]{2,1,0:T(8,128)} %param.22, f32[32,6144]{0,1:T(8,128)} %get-tuple-element.235), kind=kOutput, calls=%fused_computation.56 | convolution fusion | flops 603979776 | bytes 7110656 | tf_op jit(solution)/shard_map/jkr,lr->jkl/dot_general | solution.py:106
  231.8 70.8 %psum.14 = f32[8,32,32]{1,2,0:T(8,128)S(1)} all-reduce(f32[8,32,32]{1,2,0:T(8,128)S(1)} %fusion.20), channel_id=1, replica_groups=mesh['sec'=2,'grp'=4,'dev'=4] {'sec','grp','dev'}, use_global_device_ids=true, to_apply=%region_11.12 | all-reduce | flops 8192 | bytes 65536 | tf_op jit(solution)/shard_map/psum | solution.py:105
  302.7 7.5 %convolution_bitcast_fusion.1 = f32[32,6144]{1,0:T(8,128)S(1)} fusion(f32[8,32,32]{1,2,0:T(8,128)S(1)} %psum.14, f32[8,32,6144]{2,1,0:T(8,128)} %param.22), kind=kOutput, calls=%fused_computation.48 | convolution fusion | flops 603979776 | bytes 7110656 | tf_op jit(solution)/shard_map/jkl,jkr->lr/dot_general | solution.py:108
  310.3 16.3 %convolution_bitcast_fusion.2 = f32[8,32,32]{1,2,0:T(8,128)S(1)} fusion(f32[8,32,6144]{2,1,0:T(8,128)} %param.22, f32[32,6144]{1,0:T(8,128)S(1)} %sub.23), kind=kOutput, calls=%fused_computation.55 | convolution fusion | flops 603979776 | bytes 7110656 | tf_op jit(solution)/shard_map/jkr,lr->jkl/dot_general | solution.py:110
  326.6 41.1 %psum.15 = f32[8,32,32]{1,2,0:T(8,128)S(1)} all-reduce(f32[8,32,32]{1,2,0:T(8,128)S(1)} %convolution_bitcast_fusion.2), channel_id=1, replica_groups=mesh['sec'=2,'grp'=4,'dev'=4] {'sec','grp','dev'}, use_global_device_ids=true, to_apply=%region_12.13 | all-reduce | flops 8192 | bytes 65536 | tf_op jit(solution)/shard_map/psum | solution.py:109
  367.7 7.6 %fusion.14 = f32[32,6144]{1,0:T(8,128)S(1)} fusion(f32[32,6144]{1,0:T(8,128)S(1)} %sub.23, f32[8,32,32]{1,2,0:T(8,128)S(1)} %psum.15, f32[8,32,6144]{2,1,0:T(8,128)} %param.22), kind=kOutput, calls=%fused_computation.49 | convolution fusion | flops 604176384 | bytes 7897088 | tf_op jit(solution)/shard_map/jkl,jkr->lr/dot_general | solution.py:112
  376.1 77.8 %all-gather = f32[1024,32]{1,0:T(8,128)S(1)} all-gather(f32[32,32]{1,0:T(8,128)S(1)} %fusion.38), channel_id=2, replica_groups=mesh['sec'=2,'grp'=4,'dev'=4] {'sec','grp','dev'}, dimensions={0}, use_global_device_ids=true | all-gather | bytes 135168 | tf_op jit(solution)/shard_map/all_gather | solution.py:115
  454.2 2.9 cholesky.16
  458.4 2.4 custom-call.6
  460.9 1.7 fusion.30
  (52 shorter events, 11.5 us)
Async XLA Ops:
  23.1 35.7 %all-to-all-start = ((f32[32,1,392]{2,1,0:T(1,128)}), f32[32,1,392]{2,1,0:T(1,128)S(1)}, u32[]{:S(2)}, u32[]{:S(2)}) async-start(f32[32,1,392]{2,1,0:T(1,128)} %all_to_all.9), calls=%async_computation | async-start | bytes 131072 | tf_op jit(solution)/shard_map/all_to_all | solution.py:80
  58.8 5.9 %copy-start = (f32[32,6144]{1,0:T(8,128)S(1)}, f32[32,6144]{1,0:T(8,128)}, u32[]{:S(2)}) copy-start(f32[32,6144]{1,0:T(8,128)} %param.21) | copy-start | bytes 2359300
  58.8 66.9 %copy-start.3 = (f32[1,4,1536]{2,1,0:T(4,128)S(1)}, f32[1,4,1536]{2,1,0:T(4,128)}, u32[]{:S(2)}) copy-start(f32[1,4,1536]{2,1,0:T(4,128)} %param.26) | copy-start | bytes 73732
  58.8 66.9 %copy-start.4 = (s32[1,4,1536]{2,1,0:T(4,128)S(1)}, s32[1,4,1536]{2,1,0:T(4,128)}, u32[]{:S(2)}) copy-start(s32[1,4,1536]{2,1,0:T(4,128)} %param.25) | copy-start | bytes 73732
  58.8 66.9 %copy-start.5 = (f32[6144]{0:T(1024)S(1)}, f32[6144]{0:T(1024)}, u32[]{:S(2)}) copy-start(f32[6144]{0:T(1024)} %param.27) | copy-start | bytes 73732
  58.8 66.9 %copy-start.6 = (s32[64,6]{0,1:T(8,128)S(1)}, s32[64,6]{0,1:T(8,128)}, u32[]{:S(2)}) copy-start(s32[64,6]{0,1:T(8,128)} %param.24) | copy-start | bytes 4612
  58.8 66.8 %all-to-all-start.1 = ((f32[32,32,392]{2,1,0:T(8,128)}), f32[32,32,392]{2,1,0:T(8,128)S(1)}, u32[]{:S(2)}, u32[]{:S(2)}) async-start(f32[32,32,392]{2,1,0:T(8,128)} %copy.122), calls=%async_computation.1 | async-start | bytes 4194304 | tf_op jit(solution)/shard_map/all_to_all | solution.py:79
  65.4 60.2 %collective-permute-start.2 = (f32[32,1536]{1,0:T(8,128)}, f32[32,1536]{1,0:T(8,128)}, u32[]{:S(2)}, u32[]{:S(2)}) collective-permute-start(f32[32,1536]{1,0:T(8,128)} %get-tuple-element.226), channel_id=1, source_target_pairs={{0,1},{1,0},{2,3},{3,2},{4,5},{5,4},{6,7},{7,6},{8,9},{9,8},{10,11... | collective-permute-start | bytes 589832 | tf_op jit(solution)/shard_map/ppermute | solution.py:18
  66.9 58.7 %collective-permute-start.3 = (f32[32,1536]{1,0:T(8,128)}, f32[32,1536]{1,0:T(8,128)}, u32[]{:S(2)}, u32[]{:S(2)}) collective-permute-start(f32[32,1536]{1,0:T(8,128)} %get-tuple-element.225), channel_id=1, source_target_pairs={{0,2},{2,0},{1,3},{3,1},{4,6},{6,4},{5,7},{7,5},{8,10},{10,8},{9,1... | collective-permute-start | bytes 589832 | tf_op jit(solution)/shard_map/ppermute | solution.py:18
  69.3 56.3 %collective-permute-start.4 = (f32[32,1536]{1,0:T(8,128)S(1)}, f32[32,1536]{1,0:T(8,128)}, u32[]{:S(2)}, u32[]{:S(2)}) collective-permute-start(f32[32,1536]{1,0:T(8,128)S(1)} %get-tuple-element.224), channel_id=1, source_target_pairs={{0,4},{4,0},{8,12},{12,8},{1,5},{5,1},{9,13},{13,9},{2,6},{6,2},{1... | collective-permute-start | bytes 589832 | tf_op jit(solution)/shard_map/ppermute | solution.py:18
  70.8 54.8 %collective-permute-start.5 = (f32[32,1536]{1,0:T(8,128)S(1)}, f32[32,1536]{1,0:T(8,128)}, u32[]{:S(2)}, u32[]{:S(2)}) collective-permute-start(f32[32,1536]{1,0:T(8,128)S(1)} %get-tuple-element.223), channel_id=1, source_target_pairs={{0,8},{8,0},{4,12},{12,4},{1,9},{9,1},{5,13},{13,5},{2,10},{10,2},... | collective-permute-start | bytes 589832 | tf_op jit(solution)/shard_map/ppermute | solution.py:18
  71.4 41.1 %collective-permute-start = (f32[32,1]{1,0:T(8,128)S(1)}, f32[32,1]{1,0:T(8,128)S(1)}, u32[]{:S(2)}, u32[]{:S(2)}) collective-permute-start(f32[32,1]{1,0:T(8,128)S(1)} %get-tuple-element.228), channel_id=1, source_target_pairs={{0,1},{1,2},{2,3},{3,4},{4,5},{5,6},{6,7},{7,8},{8,9},{9,10},{10,1... | collective-permute-start | bytes 392 | tf_op jit(solution)/shard_map/ppermute | solution.py:28
  112.5 11.9 %collective-permute-start.1 = (f32[32,1]{1,0:T(8,128)S(1)}, f32[32,1]{1,0:T(8,128)S(1)}, u32[]{:S(2)}, u32[]{:S(2)}) collective-permute-start(f32[32,1]{1,0:T(8,128)S(1)} %get-tuple-element.227), channel_id=1, source_target_pairs={{1,0},{2,1},{3,2},{4,3},{5,4},{6,5},{7,6},{8,7},{9,8},{10,9},{11,1... | collective-permute-start | bytes 392 | tf_op jit(solution)/shard_map/ppermute | solution.py:29
